TPU v7x, 256 devices: a whole 4x4x8 slice. The times are simulated.
256 devices in a mesh: buoy: 4 (over x), dom: 64 (over z, y, core).
Axes of the slice: x: 4, y: 4, z: 8, core: 2. Of those that a mesh axis runs over, the one named last changes fastest.
Arguments:
- ambient: float32 [32, 36, 448], P('buoy', None, 'dom'), may hold values from -6 to 6
- initial_out: float32 [32, 36, 448], P('buoy', None, 'dom'), may hold values from -6 to 6
- translation: bfloat16 [512, 448, 448], P(('buoy', 'dom')), may hold values from -0.0625 to 0.0625
- pair_source: int32 [512], P(('buoy', 'dom')), may hold values from 0 to 31, as said below
- pair_target: int32 [512], P(('buoy', 'dom')), may hold values from 0 to 31, as said below
- pair_live: int32 [512], P(('buoy', 'dom')), may hold values from 0 to 1, as said below
- diffract: bfloat16 [448, 448], P('dom'), may hold values from -0.25 to 0.25
- panel_rows: bfloat16 [8192, 448], P('dom'), may hold values from -0.25 to 0.25
Outputs:
- outgoing: float32 [32, 36, 448], P('buoy', None, 'dom')
- sources: bfloat16 [32, 36, 8192], P('buoy', None, 'dom')
Inputs may be any that keep to these rules, and one draw needn't show every extreme that they name: `pair_target`: the slots of one device name target buoys among the 8 buoys of its index of buoy. `pair_source`: A source buoy differs from its target by 1 to 8 places in the farm's order; the live slots of one target name distinct sources. `pair_live`: A slot is live exactly where its source lies inside the farm; some device has all 2 live.
All inputs are finite; a program needn't handle non-finite values.
Results may differ from a plain program's by a relative error of at most 0.015.
Values may be sent and summed in bfloat16 or wider, within the bound.
No kernel may reach another device: no remote copies, remote signals or barrier semaphores. Data moves between devices by JAX's collectives and lax.ppermute only.
A program may use at most 64 MiB of HBM per device.

v0:
```python
import jax
import jax.numpy as jnp
from jax import lax
from jax.sharding import PartitionSpec as P

ITERS = 2


def extended_2(block, sides, width):
    for axis, dim in sides:
        count = lax.axis_size(axis)
        forward = [(i, i + 1) for i in range(count - 1)]
        backward = [(target, source) for source, target in forward]
        low = lax.ppermute(
            lax.slice_in_dim(block, block.shape[dim] - width, None, axis=dim), axis, forward
        )
        high = lax.ppermute(lax.slice_in_dim(block, 0, width, axis=dim), axis, backward)
        block = jnp.concatenate([low, block, high], axis=dim)
    return block


def rows_product(left, right):
    return lax.dot_general(
        left, right, (((1,), (1,)), ((), ())), preferred_element_type=jnp.float32
    )


def shards(
    ambient, initial_out, translation, pair_source, pair_target, pair_live, diffract, panel_rows
):
    per_dev, headings, share_width = initial_out.shape
    full_width = translation.shape[1]
    first_buoy = lax.axis_index("buoy") * per_dev
    column_start = lax.axis_index("dom") * share_width
    rows_source = pair_source - (first_buoy - per_dev)
    rows_target = pair_target - first_buoy
    place_table = (
        (rows_target[None, :] == jnp.arange(per_dev, dtype=jnp.int32)[:, None])
        & (pair_live[None, :] == 1)
    ).astype(jnp.float32)
    matrices = translation.astype(jnp.float32)
    coeffs = initial_out
    incident_bf = None
    for step in range(ITERS):
        whole = lax.all_gather(coeffs, "dom", axis=2, tiled=True)
        extended = extended_2(whole.astype(jnp.bfloat16), (("buoy", 0),), per_dev).astype(
            whole.dtype
        )
        picked = jnp.take(extended, rows_source, axis=0)
        terms = jnp.einsum("phn,pmn->phm", picked, matrices, precision=lax.Precision.HIGHEST)
        partial_value = jnp.einsum(
            "kp,phm->khm", place_table, terms, precision=lax.Precision.HIGHEST
        )
        own_columns = (
            lax.dynamic_slice_in_dim(partial_value, column_start, share_width, 2) + ambient
        )
        partial_value = lax.dynamic_update_slice_in_dim(partial_value, own_columns, column_start, 2)
        incident = lax.psum(partial_value, "dom")
        incident_bf = incident.astype(jnp.bfloat16)
        flat = incident_bf.reshape(per_dev * headings, full_width)
        coeffs = rows_product(flat, diffract).reshape(per_dev, headings, share_width)
    flat = incident_bf.reshape(per_dev * headings, full_width)
    sources = (
        rows_product(flat, panel_rows)
        .astype(jnp.bfloat16)
        .reshape(per_dev, headings, panel_rows.shape[0])
    )
    return (coeffs, sources)


def solution(mesh):
    in_specs = (
        P("buoy", None, "dom"),
        P("buoy", None, "dom"),
        P(("buoy", "dom"), None, None),
        P(("buoy", "dom")),
        P(("buoy", "dom")),
        P(("buoy", "dom")),
        P("dom", None),
        P("dom", None),
    )
    out_specs = (P("buoy", None, "dom"), P("buoy", None, "dom"))
    return jax.shard_map(shards, mesh=mesh, in_specs=in_specs, out_specs=out_specs, check_vma=False)
```

profile of v0, /device:TPU:6, one launch (start us, length us, event | category | flops | bytes accessed | tf_op | source)
XLA Modules:
  0.0 659.2 jit_solution(17983448239093237719)
XLA Ops:
  0.7 0.8 convert.2
  1.5 53.9 %all_gather.6 = bf16[8,36,448]{1,0,2:T(8,128)(2,1)S(1)} all-gather(bf16[8,36,7]{1,0,2:T(8,128)(2,1)S(1)} %convert.2), channel_id=1, replica_groups=mesh['buoy'=4,'dom'=64] {'dom'}, dimensions={2}, use_global_device_ids=true | all-gather | bytes 262080 | tf_op jit(solution)/shard_map/all_gather | solution.py:45
  55.4 0.7 copy.70
  56.1 2.7 collective-permute-start.1
  58.9 1.3 collective-permute-start
  60.4 5.9 collective-permute-done.1
  66.3 0.7 copy-done.1
  67.0 3.5 collective-permute-done
  70.6 1.3 maximum_convert_fusion
  72.4 0.9 fusion.4
  74.0 0.6 dynamic_update_slice.6
  74.6 258.2 %all-reduce.2 = bf16[8,36,448]{2,0,1:T(8,128)(2,1)S(1)} all-reduce(f32[8,36,448]{2,0,1:T(8,128)S(1)} %dynamic_update_slice.6), channel_id=1, replica_groups=mesh['buoy'=4,'dom'=64] {'dom'}, use_global_device_ids=true, to_apply=%region_0.0 | all-reduce | flops 129024 | bytes 774144 | tf_op jit(solution)/shard_map/psum | solution.py:58
  333.2 47.3 %all_gather.7 = bf16[8,36,448]{1,0,2:T(8,128)(2,1)S(1)} all-gather(bf16[8,36,7]{1,0,2:T(8,128)(2,1)S(1)} %copy.74), channel_id=1, replica_groups=mesh['buoy'=4,'dom'=64] {'dom'}, dimensions={2}, use_global_device_ids=true | all-gather | bytes 262080 | tf_op jit(solution)/shard_map/all_gather | solution.py:45
  380.5 0.9 copy.75
  381.4 2.4 collective-permute-start.3
  383.9 1.5 collective-permute-start.2
  385.3 5.3 collective-permute-done.3
  390.6 4.1 collective-permute-done.2
  395.0 1.0 copy.76
  396.6 0.9 fusion.2
  398.2 0.6 dynamic_update_slice.7
  398.8 258.3 %all-reduce.3 = bf16[8,36,448]{2,0,1:T(8,128)(2,1)S(1)} all-reduce(f32[8,36,448]{2,0,1:T(8,128)S(1)} %dynamic_update_slice.7), channel_id=1, replica_groups=mesh['buoy'=4,'dom'=64] {'dom'}, use_global_device_ids=true, to_apply=%region_1.3 | all-reduce | flops 129024 | bytes 774144 | tf_op jit(solution)/shard_map/psum | solution.py:58
  657.5 0.6 copy.81
  658.5 0.6 copy.82
  (34 shorter events, 4.0 us)
Async XLA Ops:
  0.6 71.8 %copy-start = (bf16[2,448,448]{2,1,0:T(8,128)(2,1)S(1)}, bf16[2,448,448]{2,1,0:T(8,128)(2,1)}, u32[]{:S(2)}) copy-start(bf16[2,448,448]{2,1,0:T(8,128)(2,1)} %param.12) | copy-start | bytes 2408452
  0.6 59.5 %copy-start.6 = (s32[2]{0:T(128)S(1)}, s32[2]{0:T(128)}, u32[]{:S(2)}) copy-start(s32[2]{0:T(128)} %param.14) | copy-start | bytes 28
  0.7 59.5 %copy-start.4 = (s32[2]{0:T(128)S(1)}, s32[2]{0:T(128)}, u32[]{:S(2)}) copy-start(s32[2]{0:T(128)} %param.13) | copy-start | bytes 28
  0.7 59.6 %copy-start.3 = (f32[8,36,7]{1,0,2:T(8,128)S(1)}, f32[8,36,7]{1,0,2:T(8,128)}, u32[]{:S(2)}) copy-start(f32[8,36,7]{1,0,2:T(8,128)} %param.10) | copy-start | bytes 24196
  0.7 59.7 %copy-start.7 = (s32[2]{0:T(128)S(1)}, s32[2]{0:T(128)}, u32[]{:S(2)}) copy-start(s32[2]{0:T(128)} %param.15) | copy-start | bytes 28
  56.1 10.2 %collective-permute-start.1 = (bf16[8,36,448]{2,1,0:T(8,128)(2,1)S(1)}, bf16[8,36,448]{2,1,0:T(8,128)(2,1)S(1)}, u32[]{:S(2)}, u32[]{:S(2)}) collective-permute-start(bf16[8,36,448]{2,1,0:T(8,128)(2,1)S(1)} %copy.70), channel_id=1, source_target_pairs={{64,0},{128,64},{192,128},{65,1},{129,65},{193,129},{66,2},{130,66... | collective-permute-start | bytes 774152 | tf_op jit(solution)/shard_map/ppermute | solution.py:17
  58.9 11.7 %collective-permute-start = (bf16[8,36,448]{2,1,0:T(8,128)(2,1)S(1)}, bf16[8,36,448]{2,1,0:T(8,128)(2,1)}, u32[]{:S(2)}, u32[]{:S(2)}) collective-permute-start(bf16[8,36,448]{2,1,0:T(8,128)(2,1)S(1)} %copy.70), channel_id=1, source_target_pairs={{0,64},{64,128},{128,192},{1,65},{65,129},{129,193},{2,66},{66,130... | collective-permute-start | bytes 774152 | tf_op jit(solution)/shard_map/ppermute | solution.py:14
  66.3 0.7 copy-start.1
  72.4 260.5 %copy-start.5 = (bf16[7,448]{1,0:T(8,128)(2,1)S(1)}, bf16[7,448]{1,0:T(8,128)(2,1)}, u32[]{:S(2)}) copy-start(bf16[7,448]{1,0:T(8,128)(2,1)} %param.16) | copy-start | bytes 18820
  381.4 9.2 %collective-permute-start.3 = (bf16[8,36,448]{2,0,1:T(8,128)(2,1)S(1)}, bf16[8,36,448]{2,0,1:T(8,128)(2,1)S(1)}, u32[]{:S(2)}, u32[]{:S(2)}) collective-permute-start(bf16[8,36,448]{2,0,1:T(8,128)(2,1)S(1)} %copy.75), channel_id=1, source_target_pairs={{64,0},{128,64},{192,128},{65,1},{129,65},{193,129},{66,2},{130,66... | collective-permute-start | bytes 774152 | tf_op jit(solution)/shard_map/ppermute | solution.py:17
  383.9 10.9 %collective-permute-start.2 = (bf16[8,36,448]{2,0,1:T(8,128)(2,1)S(1)}, bf16[8,36,448]{2,0,1:T(8,128)(2,1)S(1)}, u32[]{:S(2)}, u32[]{:S(2)}) collective-permute-start(bf16[8,36,448]{2,0,1:T(8,128)(2,1)S(1)} %copy.75), channel_id=1, source_target_pairs={{0,64},{64,128},{128,192},{1,65},{65,129},{129,193},{2,66},{66,130... | collective-permute-start | bytes 774152 | tf_op jit(solution)/shard_map/ppermute | solution.py:14
  398.1 260.2 %copy-start.2 = (bf16[128,448]{0,1:T(8,128)(2,1)S(1)}, bf16[128,448]{0,1:T(8,128)(2,1)}, u32[]{:S(2)}) copy-start(bf16[128,448]{0,1:T(8,128)(2,1)} %param.17) | copy-start | bytes 344068
where the time goes:
time: 659 us
  blocking collectives  618 us (94%)
  waiting for transfers between devices  18.8 us (3%)
  starting transfers between devices  7.95 us (1%)
  local copies, waits for them, and re-layouts  7.34 us (1%)
    psum x2, blocking collectives, shards(): incident = lax.psum(partial_value, 'dom')  517 us
    all_gather x2, blocking collectives, shards(): whole = lax.all_gather(coeffs, 'dom', axis=2, tiled=True)  101 us
  transfers between devices with their start and end apart: 4, of which 4 were waited for; matrix products, arithmetic and copies ran while one was open for 0% of the time, Pallas kernels for 0%

commit v1 on v0

--- a/solution.py
+++ b/solution.py
@@ -4,6 +4,12 @@
 from jax.sharding import PartitionSpec as P
 
 ITERS = 2
+
+
+def summed_here(array, name):
+    blocks = lax.all_gather(array, name, axis=0, tiled=False)
+    summed = blocks.sum(axis=0)
+    return summed
 
 
 def extended_2(block, sides, width):
@@ -55,7 +61,7 @@
             lax.dynamic_slice_in_dim(partial_value, column_start, share_width, 2) + ambient
         )
         partial_value = lax.dynamic_update_slice_in_dim(partial_value, own_columns, column_start, 2)
-        incident = lax.psum(partial_value, "dom")
+        incident = summed_here(partial_value, "dom")
         incident_bf = incident.astype(jnp.bfloat16)
         flat = incident_bf.reshape(per_dev * headings, full_width)
         coeffs = rows_product(flat, diffract).reshape(per_dev, headings, share_width)

time: 659 us -> 499 us (0.76)
  blocking collectives: 618 us -> 103 us
  waiting for transfers between devices: 18.8 us -> 329 us
  other arithmetic: 2.58 us -> 29.8 us
  between operations: 0.97 us -> 14.4 us
    psum x2 -> x0, blocking collectives: 517 us -> none  [shards(): incident = lax.psum(partial_value, 'dom')]
    all_gather x0 -> x2, waiting for transfers between devices: none -> 311 us  [summed_here(): blocks = lax.all_gather(array, name, axis=0, tiled=False)]
    reduce_sum x0 -> x2, other arithmetic: none -> 27.3 us  [summed_here(): summed = blocks.sum(axis=0)]
  transfers between devices with their start and end apart: 4 -> 6, of which waited for: 4 -> 6; matrix products, arithmetic and copies ran while one was open for 0% -> 0% of each run, Pallas kernels for 0% -> 0%
where the time goes in v1:
time: 499 us; the launch traced here: 497 us
  waiting for transfers between devices  329 us (66%)
  blocking collectives  103 us (21%)
  other arithmetic  29.8 us (6%)
  between operations  14.4 us (3%)
  local copies, waits for them, and re-layouts  8.95 us (2%)
  starting transfers between devices  8.36 us (2%)
    all_gather x2, waiting for transfers between devices, summed_here(): blocks = lax.all_gather(array, name, axis=0, tiled=False)  311 us
    all_gather x2, blocking collectives, shards(): whole = lax.all_gather(coeffs, 'dom', axis=2, tiled=True)  103 us
    reduce_sum x2, other arithmetic, summed_here(): summed = blocks.sum(axis=0)  27.3 us
    ppermute x2, waiting for transfers between devices, extended_2(): lax.ppermute(lax.slice_in_dim(block, 0, width, axis=dim), axis, backward)  11.1 us
  transfers between devices with their start and end apart: 6, of which 6 were waited for; matrix products, arithmetic and copies ran while one was open for 0% of the time, Pallas kernels for 0%

profile of v1, /device:TPU:6, one launch (start us, length us, event | category | flops | bytes accessed | tf_op | source)
XLA Modules:
  0.0 497.4 jit_solution(6649758735471909923)
XLA Ops:
  7.3 0.8 convert.2
  8.1 53.9 %all_gather.22 = bf16[8,36,448]{1,0,2:T(8,128)(2,1)S(1)} all-gather(bf16[8,36,7]{1,0,2:T(8,128)(2,1)S(1)} %convert.2), channel_id=1, replica_groups=mesh['buoy'=4,'dom'=64] {'dom'}, dimensions={2}, use_global_device_ids=true | all-gather | bytes 262080 | tf_op jit(solution)/shard_map/all_gather | solution.py:51
  62.0 0.7 copy.65
  62.7 2.7 collective-permute-start.1
  65.4 1.3 collective-permute-start
  67.0 5.9 %collective-permute-done.1 = bf16[8,36,448]{2,1,0:T(8,128)(2,1)S(1)} collective-permute-done((bf16[8,36,448]{2,1,0:T(8,128)(2,1)S(1)}, bf16[8,36,448]{2,1,0:T(8,128)(2,1)S(1)}, u32[]{:S(2)}, u32[]{:S(2)}) %collective-permute-start.1) | collective-permute-done | bytes 258080 | tf_op jit(solution)/shard_map/ppermute | solution.py:23
  72.9 0.7 copy-done.4
  73.6 3.5 collective-permute-done
  77.1 1.3 maximum_convert_fusion
  79.0 0.9 fusion.4
  81.2 0.8 copy-done.3
  82.1 155.0 %all-gather.3.cloned.1.call-done = f32[64,8,36,448]{3,1,2,0:T(8,128)} async-done(((f32[1,8,36,448]{3,1,2,0:T(8,128)}), f32[64,8,36,448]{3,1,2,0:T(8,128)}) %all-gather.3.cloned.1.call-update) | async-done | bytes 33030160 | tf_op jit(solution)/shard_map/all_gather | solution.py:10
  237.1 13.6 %reduce_sum.18 = bf16[8,36,448]{2,0,1:T(8,128)(2,1)S(1)} reduce(f32[64,8,36,448]{3,1,2,0:T(8,128)} %all-gather.3.cloned.1.call-done, f32[]{:T(128)} %constant.34.clone.1), dimensions={0}, to_apply=%region_0.0 | reduce | flops 8128512 | bytes 33288196 | tf_op jit(solution)/shard_map/reduce_sum | solution.py:11
  251.0 48.7 %all_gather.26 = bf16[8,36,448]{1,0,2:T(8,128)(2,1)S(1)} all-gather(bf16[8,36,7]{1,0,2:T(8,128)(2,1)S(1)} %copy.69), channel_id=1, replica_groups=mesh['buoy'=4,'dom'=64] {'dom'}, dimensions={2}, use_global_device_ids=true | all-gather | bytes 262080 | tf_op jit(solution)/shard_map/all_gather | solution.py:51
  299.7 0.9 copy.70
  300.6 2.8 collective-permute-start.3
  303.4 1.5 collective-permute-start.2
  304.9 5.3 %collective-permute-done.3 = bf16[8,36,448]{2,0,1:T(8,128)(2,1)S(1)} collective-permute-done((bf16[8,36,448]{2,0,1:T(8,128)(2,1)S(1)}, bf16[8,36,448]{2,0,1:T(8,128)(2,1)S(1)}, u32[]{:S(2)}, u32[]{:S(2)}) %collective-permute-start.3) | collective-permute-done | bytes 258080 | tf_op jit(solution)/shard_map/ppermute | solution.py:23
  310.1 4.1 collective-permute-done.2
  314.5 1.0 copy.71
  316.1 0.9 fusion.2
  318.3 0.8 copy-done.2
  319.2 155.6 %all-gather.5.cloned.1.call-done = f32[64,8,36,448]{3,1,2,0:T(8,128)} async-done(((f32[1,8,36,448]{3,1,2,0:T(8,128)}), f32[64,8,36,448]{3,1,2,0:T(8,128)}) %all-gather.5.cloned.1.call-update) | async-done | bytes 33030160 | tf_op jit(solution)/shard_map/all_gather | solution.py:10
  474.8 13.7 %reduce_sum.19 = bf16[8,36,448]{2,0,1:T(8,128)(2,1)S(1)} reduce(f32[64,8,36,448]{3,1,2,0:T(8,128)} %all-gather.5.cloned.1.call-done, f32[]{:T(128)} %constant.34.clone.1), dimensions={0}, to_apply=%region_1.3 | reduce | flops 8128512 | bytes 33288196 | tf_op jit(solution)/shard_map/reduce_sum | solution.py:11
  (46 shorter events, 6.5 us)
Async XLA Ops:
  7.2 71.8 %copy-start = (bf16[2,448,448]{2,1,0:T(8,128)(2,1)S(1)}, bf16[2,448,448]{2,1,0:T(8,128)(2,1)}, u32[]{:S(2)}) copy-start(bf16[2,448,448]{2,1,0:T(8,128)(2,1)} %param.12) | copy-start | bytes 2408452
  7.2 59.6 %copy-start.9 = (s32[2]{0:T(128)S(1)}, s32[2]{0:T(128)}, u32[]{:S(2)}) copy-start(s32[2]{0:T(128)} %param.14) | copy-start | bytes 28
  7.2 59.6 %copy-start.7 = (s32[2]{0:T(128)S(1)}, s32[2]{0:T(128)}, u32[]{:S(2)}) copy-start(s32[2]{0:T(128)} %param.13) | copy-start | bytes 28
  7.2 59.6 %copy-start.6 = (f32[8,36,7]{1,0,2:T(8,128)S(1)}, f32[8,36,7]{1,0,2:T(8,128)}, u32[]{:S(2)}) copy-start(f32[8,36,7]{1,0,2:T(8,128)} %param.10) | copy-start | bytes 24196
  7.2 59.8 %copy-start.10 = (s32[2]{0:T(128)S(1)}, s32[2]{0:T(128)}, u32[]{:S(2)}) copy-start(s32[2]{0:T(128)} %param.15) | copy-start | bytes 28
  7.2 229.9 %all-gather.3.cloned.1.call-start = ((), (), s32[]{:S(2)}) async-start(), calls=%async_computation | async-start | bytes 38338560 | tf_op jit(solution)/shard_map/all_gather | solution.py:10
  62.7 10.2 %collective-permute-start.1 = (bf16[8,36,448]{2,1,0:T(8,128)(2,1)S(1)}, bf16[8,36,448]{2,1,0:T(8,128)(2,1)S(1)}, u32[]{:S(2)}, u32[]{:S(2)}) collective-permute-start(bf16[8,36,448]{2,1,0:T(8,128)(2,1)S(1)} %copy.65), channel_id=1, source_target_pairs={{64,0},{128,64},{192,128},{65,1},{129,65},{193,129},{66,2},{130,66... | collective-permute-start | bytes 774152 | tf_op jit(solution)/shard_map/ppermute | solution.py:23
  65.4 11.7 %collective-permute-start = (bf16[8,36,448]{2,1,0:T(8,128)(2,1)S(1)}, bf16[8,36,448]{2,1,0:T(8,128)(2,1)}, u32[]{:S(2)}, u32[]{:S(2)}) collective-permute-start(bf16[8,36,448]{2,1,0:T(8,128)(2,1)S(1)} %copy.65), channel_id=1, source_target_pairs={{0,64},{64,128},{128,192},{1,65},{65,129},{129,193},{2,66},{66,130... | collective-permute-start | bytes 774152 | tf_op jit(solution)/shard_map/ppermute | solution.py:20
  72.9 0.7 copy-start.4
  81.2 0.8 copy-start.3
  82.0 168.7 %copy-start.8 = (bf16[7,448]{1,0:T(8,128)(2,1)S(1)}, bf16[7,448]{1,0:T(8,128)(2,1)}, u32[]{:S(2)}) copy-start(bf16[7,448]{1,0:T(8,128)(2,1)} %param.16) | copy-start | bytes 18820
  82.0 392.8 %all-gather.5.cloned.1.call-start = ((), (), s32[]{:S(2)}) async-start(), calls=%async_computation.1 | async-start | bytes 38338560 | tf_op jit(solution)/shard_map/all_gather | solution.py:10
  300.6 9.5 %collective-permute-start.3 = (bf16[8,36,448]{2,0,1:T(8,128)(2,1)S(1)}, bf16[8,36,448]{2,0,1:T(8,128)(2,1)S(1)}, u32[]{:S(2)}, u32[]{:S(2)}) collective-permute-start(bf16[8,36,448]{2,0,1:T(8,128)(2,1)S(1)} %copy.70), channel_id=1, source_target_pairs={{64,0},{128,64},{192,128},{65,1},{129,65},{193,129},{66,2},{130,66... | collective-permute-start | bytes 774152 | tf_op jit(solution)/shard_map/ppermute | solution.py:23
  303.4 10.9 %collective-permute-start.2 = (bf16[8,36,448]{2,0,1:T(8,128)(2,1)S(1)}, bf16[8,36,448]{2,0,1:T(8,128)(2,1)S(1)}, u32[]{:S(2)}, u32[]{:S(2)}) collective-permute-start(bf16[8,36,448]{2,0,1:T(8,128)(2,1)S(1)} %copy.70), channel_id=1, source_target_pairs={{0,64},{64,128},{128,192},{1,65},{65,129},{129,193},{2,66},{66,130... | collective-permute-start | bytes 774152 | tf_op jit(solution)/shard_map/ppermute | solution.py:20
  318.3 0.8 copy-start.2
  319.2 170.4 %copy-start.5 = (bf16[128,448]{0,1:T(8,128)(2,1)S(1)}, bf16[128,448]{0,1:T(8,128)(2,1)}, u32[]{:S(2)}) copy-start(bf16[128,448]{0,1:T(8,128)(2,1)} %param.17) | copy-start | bytes 344068
  474.8 15.7 %copy-start.1 = (bf16[2,448,448]{2,1,0:T(8,128)(2,1)S(1)}, bf16[2,448,448]{2,1,0:T(8,128)(2,1)}, u32[]{:S(2)}) copy-start(bf16[2,448,448]{2,1,0:T(8,128)(2,1)} %param.12) | copy-start | bytes 2408452
Sparse Core Ops, SparseCore 0:
  82.2 154.9 all-gather.2
  319.3 155.4 all-gather.4
